TPU v7x, 128 devices: a whole 4x4x4 slice. The times are simulated.
128 devices in a mesh: gz: 16 (over y_lo, x, core), gy: 8 (over z, y_hi).
Axes of the slice: x: 4, y: 4 (y_hi: 2, y_lo: 2; y = y_hi * 2 + y_lo), z: 4, core: 2. Of those that a mesh axis runs over, the one named last changes fastest.
Arguments:
- fields: bfloat16 [6, 128, 256, 256], P(None, 'gz', 'gy'), may hold values from -13 to 13
- target: bfloat16 [128, 64, 128, 128], P(None, 'gz', 'gy'), may hold values from -6 to 6
- conv_weight: bfloat16 [64, 162], replicated, may hold values from -0.5 to 0.5
- conv_bias: float32 [64], replicated, may hold values from -3 to 3
- down_weight: bfloat16 [128, 512], replicated, may hold values from -0.25 to 0.25
- down_bias: float32 [128], replicated, may hold values from -3 to 3
Outputs:
- out_field: bfloat16 [128, 64, 128, 128], P(None, 'gz', 'gy')
- sensitivity: float32 [6, 128, 256, 256], P(None, 'gz', 'gy')
- grad_conv: float32 [64, 162], replicated
- grad_conv_bias: float32 [64], replicated
- grad_down: float32 [128, 512], P('gz')
- grad_down_bias: float32 [128], replicated
- loss: float32 [], replicated
All inputs are finite; a program needn't handle non-finite values.
Results may differ from a plain program's by a relative error of at most 0.0046.
Values may be sent and summed in bfloat16 or wider, within the bound.
A program may use at most 192 MiB of HBM per device.

v0:
```python
import jax
import jax.numpy as jnp
from jax import lax
from jax.sharding import PartitionSpec as P

gelu_scale = 0.7978845608028654
gelu_cubic = 0.044715


def with_halo(value, sides, width):
    for axis, dim in sides:
        count, length = (lax.axis_size(axis), value.shape[dim])
        up = [(i, (i + 1) % count) for i in range(count)]
        down = [(j, i) for i, j in up]
        last = lax.slice_in_dim(value, length - width, length, axis=dim)
        initial = lax.slice_in_dim(value, 0, width, axis=dim)
        before = lax.ppermute(last, axis, up)
        after = lax.ppermute(initial, axis, down)
        value = jnp.concatenate([before, value, after], axis=dim)
    return value


def shifted(value, axis, by):
    count = lax.axis_size(axis)
    return lax.ppermute(value, axis, [(i, (i + by) % count) for i in range(count)])


def gelu_parts(inputs):
    inner_arg = gelu_scale * (inputs + gelu_cubic * inputs * inputs * inputs)
    tangent = jnp.tanh(inner_arg)
    result = 0.5 * inputs * (1.0 + tangent)
    slopes = 0.5 * (1.0 + tangent) + 0.5 * inputs * (1.0 - tangent * tangent) * gelu_scale * (
        1.0 + 3.0 * gelu_cubic * inputs * inputs
    )
    return (result, slopes)


def tap_place(off_z, off_y, off_x, par_z, par_y, par_x):
    plane_slot = par_z + off_z
    row_sum = par_y + off_y
    col_sum = par_x + off_x - 1
    return (plane_slot, row_sum % 2, row_sum // 2, col_sum % 2, col_sum // 2)


def parity_columns(planes, half_rows):
    channels = planes.shape[0]
    taps = []
    for off_z in range(3):
        for off_y in range(3):
            for off_x in range(3):
                classes = []
                for par_z in range(2):
                    for par_y in range(2):
                        for par_x in range(2):
                            plane_slot, row_par, row_start, col_par, col_step = tap_place(
                                off_z, off_y, off_x, par_z, par_y, par_x
                            )
                            piece = planes[
                                :,
                                plane_slot,
                                row_par,
                                row_start : row_start + half_rows,
                                col_par,
                                :,
                            ]
                            classes.append(jnp.roll(piece, -col_step, axis=2))
                taps.append(jnp.stack(classes, axis=1))
    stacked = jnp.stack(taps, axis=1)
    return stacked.reshape(channels * 27, -1)


def parity_window(spread):
    groups = {}
    for off_z in range(3):
        for off_y in range(3):
            for off_x in range(3):
                tap_index = 9 * off_z + 3 * off_y + off_x
                for par_z in range(2):
                    for par_y in range(2):
                        for par_x in range(2):
                            plane_slot, row_par, row_start, col_par, col_step = tap_place(
                                off_z, off_y, off_x, par_z, par_y, par_x
                            )
                            piece = spread[:, tap_index, 4 * par_z + 2 * par_y + par_x]
                            piece = jnp.roll(piece, col_step, axis=2)
                            piece = jnp.pad(piece, ((0, 0), (row_start, 1 - row_start), (0, 0)))
                            slot_key = (plane_slot, row_par, col_par)
                            if slot_key in groups:
                                groups[slot_key] = groups[slot_key] + piece
                            else:
                                groups[slot_key] = piece
    by_plane = []
    for plane_slot in range(4):
        by_row = []
        for row_par in range(2):
            by_row.append(
                jnp.stack([groups[plane_slot, row_par, col_par] for col_par in range(2)], axis=2)
            )
        by_plane.append(jnp.stack(by_row, axis=1))
    return jnp.stack(by_plane, axis=1)


def on_device(fields, target, conv_weight, conv_bias, down_weight, down_bias):
    channels, depth_local, row_count, col_count = fields.shape
    hidden_count = conv_weight.shape[0]
    out_count = down_weight.shape[0]
    half_rows = row_count // 2
    half_cols = col_count // 2
    padded = with_halo(fields, (("gz", 1), ("gy", 2)), 1)
    split_in = padded.reshape(channels, depth_local + 2, half_rows + 1, 2, half_cols, 2).transpose(
        0, 1, 3, 2, 5, 4
    )
    cell_total = (
        depth_local // 2 * half_rows * half_cols * lax.axis_size("gz") * lax.axis_size("gy")
    )
    contract_rows = (((1,), (1,)), ((), ()))
    spread_mat = conv_weight.T

    def pair_step(pair_index, state_tuple):
        grad_conv, grad_cbias, grad_down, grad_dbias, square_sum, out_field, accum = state_tuple
        planes = lax.dynamic_slice_in_dim(split_in, 2 * pair_index, 4, 1)
        columns = parity_columns(planes, half_rows)
        pre_act = (
            jnp.dot(conv_weight, columns, preferred_element_type=jnp.float32) + conv_bias[:, None]
        )
        activated, slopes = gelu_parts(pre_act)
        hidden = activated.astype(jnp.bfloat16)
        blocks = hidden.reshape(hidden_count * 8, -1)
        output = (
            jnp.dot(down_weight, blocks, preferred_element_type=jnp.float32) + down_bias[:, None]
        )
        wanted = (
            lax.dynamic_index_in_dim(target, pair_index, 1, keepdims=False)
            .reshape(out_count, -1)
            .astype(jnp.float32)
        )
        diff_value = output - wanted
        grad_out = diff_value.astype(jnp.bfloat16)
        grad_down = grad_down + lax.dot_general(
            grad_out, blocks, contract_rows, preferred_element_type=jnp.float32
        )
        grad_dbias = grad_dbias + jnp.sum(diff_value, axis=1)
        back_hidden = lax.dot_general(
            down_weight, grad_out, (((0,), (0,)), ((), ())), preferred_element_type=jnp.float32
        )
        back_hidden = back_hidden.reshape(hidden_count, -1)
        grad_pre = (back_hidden * slopes).astype(jnp.bfloat16)
        grad_conv = grad_conv + lax.dot_general(
            grad_pre, columns, contract_rows, preferred_element_type=jnp.float32
        )
        grad_cbias = grad_cbias + jnp.sum(grad_pre, axis=1, dtype=jnp.float32)
        square_sum = square_sum + jnp.sum(diff_value * diff_value)
        out_piece = output.astype(jnp.bfloat16).reshape(out_count, 1, half_rows, half_cols)
        out_field = lax.dynamic_update_slice_in_dim(out_field, out_piece, pair_index, 1)
        spread = jnp.dot(spread_mat, grad_pre, preferred_element_type=jnp.float32)
        spread = spread.reshape(channels, 27, 8, half_rows, half_cols)
        window = parity_window(spread)
        current = lax.dynamic_slice_in_dim(accum, 2 * pair_index, 4, 1)
        accum = lax.dynamic_update_slice_in_dim(accum, current + window, 2 * pair_index, 1)
        return (grad_conv, grad_cbias, grad_down, grad_dbias, square_sum, out_field, accum)

    start_state = (
        jnp.zeros((hidden_count, channels * 27), jnp.float32),
        jnp.zeros((hidden_count,), jnp.float32),
        jnp.zeros((out_count, hidden_count * 8), jnp.float32),
        jnp.zeros((out_count,), jnp.float32),
        jnp.zeros((), jnp.float32),
        jnp.zeros((out_count, depth_local // 2, half_rows, half_cols), jnp.bfloat16),
        jnp.zeros((channels, depth_local + 2, 2, half_rows + 1, 2, half_cols), jnp.float32),
    )
    final_state = lax.fori_loop(0, depth_local // 2, pair_step, start_state)
    grad_conv, grad_cbias, grad_down, grad_dbias, square_sum, out_field, accum = final_state
    accum = accum.transpose(0, 1, 3, 2, 5, 4).reshape(
        channels, depth_local + 2, row_count + 2, col_count
    )
    from_above = shifted(accum[:, 0].astype(jnp.bfloat16), "gz", -1).astype(jnp.float32)
    from_below = shifted(accum[:, depth_local + 1].astype(jnp.bfloat16), "gz", 1).astype(
        jnp.float32
    )
    core = accum[:, 1 : depth_local + 1]
    core = core.at[:, depth_local - 1].add(from_above)
    core = core.at[:, 0].add(from_below)
    from_right = shifted(core[:, :, 0].astype(jnp.bfloat16), "gy", -1).astype(jnp.float32)
    from_left = shifted(core[:, :, row_count + 1].astype(jnp.bfloat16), "gy", 1).astype(jnp.float32)
    sensitivity = core[:, :, 1 : row_count + 1]
    sensitivity = sensitivity.at[:, :, row_count - 1].add(from_right)
    sensitivity = sensitivity.at[:, :, 0].add(from_left)
    down_total, conv_total, cbias_total, dbias_total, square_total = lax.psum(
        (grad_down, grad_conv, grad_cbias, grad_dbias, square_sum), ("gz", "gy")
    )
    share_rows = out_count // lax.axis_size("gz")
    down_rows = lax.dynamic_slice_in_dim(
        down_total, lax.axis_index("gz") * share_rows, share_rows, 0
    )
    return (
        out_field,
        sensitivity,
        conv_total / cell_total,
        cbias_total / cell_total,
        down_rows / cell_total,
        dbias_total / cell_total,
        square_total / (out_count * cell_total),
    )


def solution(mesh):
    in_specs = (P(None, "gz", "gy", None), P(None, "gz", "gy", None), P(), P(), P(), P())
    out_specs = (
        P(None, "gz", "gy", None),
        P(None, "gz", "gy", None),
        P(),
        P(),
        P("gz", None),
        P(),
        P(),
    )
    return jax.shard_map(
        on_device, mesh=mesh, in_specs=in_specs, out_specs=out_specs, check_vma=False
    )
```

profile of v0, /device:TPU:0, one launch (start us, length us, event | category | flops | bytes accessed | tf_op | source)
XLA Modules:
  0.0 907.0 jit_solution(4960366681220129995)
XLA Ops:
  25.6 9.3 %copy.1180 = bf16[6,10,34,256]{1,3,2,0:T(8,128)(2,1)} copy(bf16[6,10,34,256]{3,2,1,0:T(8,128)(2,1)S(1)} %pad_maximum_fusion) | data formatting | bytes 2088960 | tf_op jit(solution)/shard_map/concatenate | solution.py:19
  35.0 26.1 %copy.1182 = bf16[6,10,2,17,2,128]{5,3,0,4,2,1:T(8,128)(2,1)} copy(bf16[6,10,2,17,2,128]{1,4,5,2,3,0:T(2,128)(2,1)} %bitcast.2044) | data formatting | bytes 2088960
  63.1 483.7 %while.32 = (s32[]{:T(128)}, f32[64,162]{1,0:T(8,128)}, f32[64]{0:T(128)S(1)}, f32[128,512]{1,0:T(8,128)S(1)}, f32[128]{0:T(128)S(1)}, /*index=5*/f32[]{:T(128)}...) while((s32[]{:T(128)}, f32[64,162]{1,0:T(8,128)}, ...), condition=%wide.region_4.5_spmd.clone, body=%wide.region_0.4_spmd.clone.sunk | while | flops 1868444032 | bytes 235068928 | solution.py:171
  116.7 9.2 %reshape.286 = bf16[162,16384]{1,0:T(8,128)(2,1)} reshape(bf16[6,27,8,16,128]{4,3,2,1,0:T(8,128)(2,1)} %copy.1421) | data formatting | bytes 10616832 | tf_op jit(solution)/shard_map/while/body/eval_jaxpr/reshape | solution.py:69
  125.9 7.3 multiply_convert_fusion.2
  161.1 6.2 copy.1424
  231.4 9.2 %reshape.286 = bf16[162,16384]{1,0:T(8,128)(2,1)} reshape(bf16[6,27,8,16,128]{4,3,2,1,0:T(8,128)(2,1)} %copy.1421) | data formatting | bytes 10616832 | tf_op jit(solution)/shard_map/while/body/eval_jaxpr/reshape | solution.py:69
  240.6 7.3 multiply_convert_fusion.2
  346.0 9.2 %reshape.286 = bf16[162,16384]{1,0:T(8,128)(2,1)} reshape(bf16[6,27,8,16,128]{4,3,2,1,0:T(8,128)(2,1)} %copy.1421) | data formatting | bytes 10616832 | tf_op jit(solution)/shard_map/while/body/eval_jaxpr/reshape | solution.py:69
  355.3 7.3 multiply_convert_fusion.2
  460.7 9.2 %reshape.286 = bf16[162,16384]{1,0:T(8,128)(2,1)} reshape(bf16[6,27,8,16,128]{4,3,2,1,0:T(8,128)(2,1)} %copy.1421) | data formatting | bytes 10616832 | tf_op jit(solution)/shard_map/while/body/eval_jaxpr/reshape | solution.py:69
  469.9 7.3 multiply_convert_fusion.2
  546.8 28.1 %copy.1184 = f32[6,10,17,2,128,2]{1,5,4,3,2,0:T(2,128)} copy(f32[6,10,17,2,128,2]{4,2,0,5,3,1:T(8,128)} %bitcast.3) | data formatting | bytes 4177920 | tf_op jit(solution)/shard_map/transpose | solution.py:173
  574.9 9.7 %convert.21 = bf16[6,10,34,256]{1,3,2,0:T(8,128)(2,1)S(1)} convert(f32[6,10,34,256]{1,3,2,0:T(8,128)} %bitcast.2041) | non-fusion elementwise | flops 522240 | bytes 3133440 | tf_op jit(solution)/shard_map/convert.8
  584.7 12.2 %slice_reduce_fusion = (bf16[6,34,256]{2,1,0:T(8,128)(2,1)S(1)}, bf16[6,34,256]{2,1,0:T(8,128)(2,1)S(1)}) fusion(bf16[6,10,34,256]{1,3,2,0:T(8,128)(2,1)S(1)} %convert.21), kind=kLoop, calls=%fused_computation.855 | loop fusion | bytes 417792 | tf_op jit(solution)/shard_map/slice | solution.py:177
  598.2 69.3 %all-reduce.216 = (f32[64,162]{1,0:T(8,128)S(1)}, f32[64]{0:T(128)S(1)}, f32[128]{0:T(128)S(1)}, f32[]{:T(128)}) all-reduce(f32[64,162]{1,0:T(8,128)S(1)} %copy-done.5, f32[64]{0:T(128)S(1)} %get-tuple-element.416, f32[128]{0:T(128)S(1)} %get-tuple-element.418, f32[]{:T(128)} %get-tuple-element.419), channel_id=1, replica_groups=mesh['gz'=16,'gy'=8] {'gz','gy'}, use_global_device_ids=true, to_apply=%region_5.6 | all-reduce | flops 10561 | bytes 84488 | tf_op jit(solution)/shard_map/psum | solution.py:188
  668.7 20.1 %slice.5873 = f32[6,1,34,256]{1,3,2,0:T(8,128)} slice(f32[6,10,34,256]{1,3,2,0:T(8,128)} %bitcast.2042), slice={[0:6], [8:9], [0:34], [0:256]} | slice | bytes 417792 | tf_op jit(solution)/shard_map/slice.3114
  688.8 20.0 %slice.5872 = f32[6,8,34,256]{1,3,2,0:T(8,128)} slice(f32[6,10,34,256]{1,3,2,0:T(8,128)} %bitcast.2043), slice={[0:6], [1:9], [0:34], [0:256]} | slice | bytes 3342336 | tf_op jit(solution)/shard_map/slice | solution.py:180
  708.8 14.5 %copy.1411 = f32[6,1,34,256]{3,1,0,2:T(1,128)S(1)} copy(f32[6,1,34,256]{1,3,2,0:T(8,128)} %slice.5873) | data formatting | bytes 417792
  723.3 14.2 %copy.1410 = f32[6,8,34,256]{3,1,0,2:T(8,128)S(1)} copy(f32[6,8,34,256]{1,3,2,0:T(8,128)} %slice.5872) | data formatting | bytes 3342336
  737.8 7.9 scatter-add.14
  746.0 7.9 scatter-add.15
  759.4 6.4 collective-permute-done.7
  767.9 129.6 %all-reduce.219.cloned.1.call-done = f32[128,512]{1,0:T(8,128)} async-done(((f32[128,512]{1,0:T(8,128)}), f32[128,512]{1,0:T(8,128)}) %all-reduce.219.cloned.1.call-update) | async-done | bytes 262160 | tf_op jit(solution)/shard_map/psum | solution.py:188
  (1169 shorter events, 412.0 us)
Async XLA Ops:
  7.2 890.3 %all-reduce.219.cloned.1.call-start = ((), (), s32[]{:S(2)}) async-start(), calls=%async_computation | async-start | bytes 524288 | tf_op jit(solution)/shard_map/psum | solution.py:188
  8.2 6.2 collective-permute-start
  8.3 7.3 collective-permute-start.1
  15.7 9.0 collective-permute-start.2
  19.1 5.7 collective-permute-start.3
  35.0 28.2 %copy-start.4 = (bf16[128,512]{1,0:T(8,128)(2,1)S(1)}, bf16[128,512]{1,0:T(8,128)(2,1)}, u32[]{:S(2)}) copy-start(bf16[128,512]{1,0:T(8,128)(2,1)} %param.20) | copy-start | bytes 393220
  136.1 7.8 copy-start.2
  154.4 5.2 copy-start.6
  181.8 5.3 copy-start.1
  250.8 7.8 copy-start.2
  269.1 5.2 copy-start.6
  296.5 5.3 copy-start.1
  365.5 7.8 copy-start.2
  383.7 5.2 copy-start.6
  411.2 5.4 copy-start.1
  480.1 7.9 copy-start.2
  498.4 5.2 copy-start.6
  525.8 5.4 copy-start.1
  546.8 28.2 %copy-start.3 = (f32[128,512]{1,0:T(8,128)}, f32[128,512]{1,0:T(8,128)S(1)}, u32[]{:S(2)}) copy-start(f32[128,512]{1,0:T(8,128)S(1)} %get-tuple-element.417) | copy-start | bytes 786436
  584.7 13.6 %copy-start.5 = (f32[64,162]{1,0:T(8,128)S(1)}, f32[64,162]{1,0:T(8,128)}, u32[]{:S(2)}) copy-start(f32[64,162]{1,0:T(8,128)} %get-tuple-element.415) | copy-start | bytes 124420
  596.9 140.6 %collective-permute-start.4 = (bf16[6,34,256]{2,1,0:T(8,128)(2,1)S(1)}, bf16[6,34,256]{2,1,0:T(8,128)(2,1)S(1)}, u32[]{:S(2)}, u32[]{:S(2)}) collective-permute-start(bf16[6,34,256]{2,1,0:T(8,128)(2,1)S(1)} %get-tuple-element.581), channel_id=1, source_target_pairs={{0,120},{8,0},{16,8},{24,16},{32,24},{40,32},{48,40},{56,48},{64,5... | collective-permute-start | bytes 313352 | tf_op jit(solution)/shard_map/ppermute | solution.py:25
  598.2 147.5 %collective-permute-start.5 = (bf16[6,34,256]{2,1,0:T(8,128)(2,1)S(1)}, bf16[6,34,256]{2,1,0:T(8,128)(2,1)S(1)}, u32[]{:S(2)}, u32[]{:S(2)}) collective-permute-start(bf16[6,34,256]{2,1,0:T(8,128)(2,1)S(1)} %get-tuple-element.580), channel_id=1, source_target_pairs={{0,8},{8,16},{16,24},{24,32},{32,40},{40,48},{48,56},{56,64},{64,7... | collective-permute-start | bytes 313352 | tf_op jit(solution)/shard_map/ppermute | solution.py:25
  754.0 5.4 collective-permute-start.6
  758.3 7.5 collective-permute-start.7
  (4 other events, 6.4 us)
Sparse Core Ops, SparseCore 0:
  757.6 139.7 all-reduce.218
where the time goes:
time: 924 us; the launch traced here: 907 us
  local copies, waits for them, and re-layouts  477 us (52%)
  waiting for transfers between devices  139 us (15%)
  matrix products  86.2 us (9%)
  other arithmetic  71.7 us (8%)
  blocking collectives  69.3 us (8%)
  loops' own time  31 us (3%)
  between operations  16.2 us (2%)
  starting transfers between devices  15.9 us (2%)
    while x288, local copies, waits for them, and re-layouts  133 us
    psum x1, waiting for transfers between devices, on_device(): lax.psum((grad_down, grad_conv, grad_cbias, grad_dbias, square_sum), ('gz...  130 us
    psum x1, blocking collectives, on_device(): lax.psum((grad_down, grad_conv, grad_cbias, grad_dbias, square_sum), ('gz...  69.3 us
    unnamed x13, local copies, waits for them, and re-layouts  59.6 us
    reshape x4, local copies, waits for them, and re-layouts, parity_columns(): return stacked.reshape(channels * 27, -1)  36.9 us
    another operation x1, loops' own time, on_device(): final_state = lax.fori_loop(0, depth_local // 2, pair_step, start_state)  31 us
    dot_general x4, matrix products, pair_step(): jnp.dot(conv_weight, columns, preferred_element_type=jnp.float32)  29.3 us
    transpose x1, local copies, waits for them, and re-layouts, on_device(): accum.transpose(0, 1, 3, 2, 5, 4)  28.1 us
  transfers between devices with their start and end apart: 9, of which 6 were waited for; matrix products, arithmetic and copies ran while one was open for 9% of the time, Pallas kernels for 0%

commit v1 on v0

v1 whole, which is shorter than its diff:
```python
import functools
import jax
import jax.numpy as jnp
from jax import lax
from jax.experimental import pallas as pl
from jax.experimental.pallas import tpu as pltpu
from jax.sharding import PartitionSpec as P

f32, bf16 = jnp.float32, jnp.bfloat16
MESH = pl.DeviceIdType.MESH
C, NZ, NY, NX = 6, 8, 32, 256
HID, OUT = 64, 128
TZ, TY = NZ + 2, NY + 2
HX = NX // 2
ROWS = 4
CELLS = ROWS * HX
SCALE = 0.7978845608028654
CUBIC = 0.044715
NT = (((1,), (1,)), ((), ()))
VMEM = pl.BlockSpec(memory_space=pltpu.VMEM)


def dot(a, b):
    return jnp.dot(a, b, preferred_element_type=f32)


def dot_nt(a, b):
    return lax.dot_general(a, b, NT, preferred_element_type=f32)


def iota(shape, dim):
    return lax.broadcasted_iota(jnp.int32, shape, dim)


def one_hot(mask):
    return jnp.where(mask, 1.0, 0.0)


def split_matrix():
    lane = iota((NX, 4 * HX), 1)
    want = lax.rem(2 * lax.rem(lane, HX) + lane // HX - 1 + NX, NX)
    return one_hot(iota((NX, 4 * HX), 0) == want).astype(bf16)


def tap_matrix(cols):
    lane = iota((C * 27, cols), 1)
    a, b = lane // 128, lax.rem(lane // 32, 4)
    ch, c = lax.rem(lane // 4, 8), lax.rem(lane, 4)
    ok = (a < 3) & (b < 3) & (c < 3) & (ch < C)
    want = jnp.where(ok, ch * 27 + 9 * a + 3 * b + c, -1)
    return one_hot(iota((C * 27, cols), 0) == want)


def column(row, n):
    eye = iota((n, n), 0) == iota((n, n), 1)
    return jnp.sum(jnp.where(eye, jnp.broadcast_to(row, (n, n)), 0.0), axis=1, keepdims=True)


def halves(x):
    hi = x.astype(bf16)
    return hi, (x - hi.astype(f32)).astype(bf16)


def compute_kernel(
    fields, zlo, zhi, ylo, yhi, corners, target, conv_w, conv_b, down_w, down_b,
    out_ref, sens, sz, sy, sc, gd, gc_out,
    split, wide, tiles, tgt, outs, wb, wbt, wdt, wtmp, db, pre, hid, gp, gc, acc, dsum, sqsum, ytmp,
):
    split[...] = split_matrix()

    def spread_rows(value, start, count, stride):
        parts = dot(value, split[...])
        for ch in range(C):
            for dx in range(4):
                wide[pl.ds(start + ch * 4 + dx, count, stride=stride), :] = parts[
                    ch * count : (ch + 1) * count, dx * HX : (dx + 1) * HX
                ]

    def plane(z, carry):
        spread_rows(fields[:, z].reshape(C * NY, NX), ((z + 1) * TY + 1) * 32, NY, 32)
        return carry

    lax.fori_loop(0, NZ, plane, 0)
    spread_rows(zlo[...].reshape(C * NY, NX), 32, NY, 32)
    spread_rows(zhi[...].reshape(C * NY, NX), ((NZ + 1) * TY + 1) * 32, NY, 32)
    spread_rows(ylo[...], TY * 32, NZ, TY * 32)
    spread_rows(yhi[...], (TY + NY + 1) * 32, NZ, TY * 32)
    for k in range(4):
        tile = (k // 2) * (NZ + 1) * TY + (k % 2) * (NY + 1)
        parts = dot(corners[k].astype(bf16), split[...])
        for dx in range(4):
            wide[pl.ds(tile * 32 + dx, 8, stride=4), :] = parts[:, dx * HX : (dx + 1) * HX]

    def cast_tiles(i, carry):
        rows = wide[pl.ds(pl.multiple_of(i * 320, 32), 320), :]
        pad = lax.rem(iota((320, HX), 0), 32) >= 24
        tiles[pl.ds(pl.multiple_of(i * 320, 32), 320), :] = jnp.where(pad, 1.0, rows).astype(bf16)
        return carry

    lax.fori_loop(0, TZ * TY // 10, cast_tiles, 0)

    def cast_target(i, carry):
        at = pl.ds(pl.multiple_of(i * 256, 256), 256)
        tgt[at, :] = target[at, :].astype(f32)
        return carry

    lax.fori_loop(0, OUT * 64 // 256, cast_target, 0)

    taps = tap_matrix(512).astype(bf16)
    base = dot(conv_w[...], taps)
    bias = column(conv_b[...], HID)
    b_hi = bias.astype(bf16).astype(f32)
    b_mid = (bias - b_hi).astype(bf16).astype(f32)
    b_lo = bias - b_hi - b_mid
    lane = iota((HID, 512), 1)
    for par in range(8):
        shift = (par // 4) * 128 + (par // 2 % 2) * 32 + par % 2
        moved = pltpu.roll(base, shift, 1) if shift else base
        moved = jnp.where(lane == 24, b_hi, moved)
        moved = jnp.where(lane == 25, b_mid, moved)
        moved = jnp.where(lane == 26, b_lo, moved)
        for q in range(4):
            wtmp[q, pl.ds(par, HID, stride=8), :] = moved[:, q * 128 : (q + 1) * 128]
    for q in range(4):
        wb[:, q * 128 : (q + 1) * 128] = wtmp[q].astype(bf16)
    row = iota((384, 512), 0)
    keep = one_hot(iota((384, 512), 1) == (row // 24) * 32 + lax.rem(row, 24)).astype(bf16)
    wbt[...] = dot_nt(keep, wb[...]).astype(bf16)
    eye = one_hot(iota((512, 512), 0) == iota((512, 512), 1)).astype(bf16)
    wdt[...] = dot_nt(eye, down_w[...]).astype(bf16)
    db[...] = jnp.broadcast_to(column(down_b[...], OUT), (OUT, HX))

    gd[...] = jnp.zeros_like(gd)
    gc[...] = jnp.zeros_like(gc)
    dsum[...] = jnp.zeros_like(dsum)
    sqsum[...] = jnp.zeros_like(sqsum)

    def clear(i, carry):
        acc[pl.ds(pl.multiple_of(i * 240, 8), 240), :] = jnp.zeros((240, HX), f32)
        return carry

    lax.fori_loop(0, TZ * TY // 10, clear, 0)

    def chunk(i, carry):
        per = 16 // ROWS
        zc = i // per
        y0 = lax.rem(i, per) * ROWS

        def window():
            cols = []
            for r in range(ROWS):
                parts = []
                for dz in range(4):
                    at = ((2 * zc + dz) * TY + 2 * (y0 + r)) * 32
                    parts.append(tiles[pl.ds(pl.multiple_of(at, 64), 128), :])
                cols.append(jnp.concatenate(parts, axis=0))
            return jnp.concatenate(cols, axis=1)

        pre[...] = dot(wb[...], window())
        for m in range(0, 512, 16):
            x = pre[m : m + 16, :]
            x2 = x * x
            t = jnp.tanh(x * (x2 * (SCALE * CUBIC) + SCALE))
            u = 0.5 * t + 0.5
            h = x * u
            hid[m : m + 16, :] = h.astype(bf16)
            pre[m : m + 16, :] = u + (h - h * u) * (x2 * (6 * SCALE * CUBIC) + 2 * SCALE)
        output = dot(down_w[...], hid[...])
        go, ds, sq = [], 0.0, 0.0
        for r in range(ROWS):
            at = pl.ds(zc * 16 + y0 + r, OUT, stride=64)
            value = output[:, r * HX : (r + 1) * HX] + db[...]
            outs[at, :] = value
            diff = value - tgt[at, :]
            ds = ds + diff
            sq = sq + diff * diff
            go.append(diff.astype(bf16))
        dsum[...] += ds
        sqsum[...] += sq
        go = jnp.concatenate(go, axis=1)
        gd[...] += dot_nt(go, hid[...])
        back = dot(wdt[...], go)
        gp[...] = (back * pre[...]).astype(bf16)
        grad = dot_nt(gp[...], window())
        for q in range(4):
            gc[q * 512 : (q + 1) * 512, :] += grad[:, q * 128 : (q + 1) * 128]
        spread = dot(wbt[...], gp[...])
        for dz in range(4):
            for k in range(2 * ROWS + 2):
                total = None
                for r in range(ROWS):
                    dy = k - 2 * r
                    if 0 <= dy < 4:
                        m = (dz * 4 + dy) * 24
                        piece = spread[m : m + 24, r * HX : (r + 1) * HX]
                        total = piece if total is None else total + piece
                at = ((2 * zc + dz) * TY + 2 * y0 + k) * 24
                at = pl.ds(pl.multiple_of(at, 8), 24)
                acc[at, :] += total
        return carry

    lax.fori_loop(0, 64 // ROWS, chunk, 0)

    def cast_out(i, carry):
        at = pl.ds(pl.multiple_of(i * 256, 256), 256)
        out_ref[at, :] = outs[at, :].astype(bf16)
        return carry

    lax.fori_loop(0, OUT * 64 // 256, cast_out, 0)

    def join(rows):
        hi, lo = halves(jnp.concatenate(rows, axis=1))
        return dot_nt(hi, split[...]) + dot_nt(lo, split[...])

    def gather(start, count, stride):
        parts = []
        for dx in range(4):
            pieces = [acc[pl.ds(start + ch * 4 + dx, count, stride=stride), :] for ch in range(C)]
            parts.append(jnp.concatenate(pieces, axis=0))
        return join(parts)

    def sens_plane(z, carry):
        value = gather(((z + 1) * TY + 1) * 24, NY, 24)
        for ch in range(C):
            at = pl.multiple_of(ch * NZ * NY + z * NY, NY)
            sens[pl.ds(at, NY), :] = value[ch * NY : (ch + 1) * NY]
        return carry

    lax.fori_loop(0, NZ, sens_plane, 0)
    sz[0] = gather(24, NY, 24).astype(bf16)
    sz[1] = gather(((NZ + 1) * TY + 1) * 24, NY, 24).astype(bf16)
    sy[0] = gather(TY * 24, NZ, TY * 24).astype(bf16)
    sy[1] = gather((TY + NY + 1) * 24, NZ, TY * 24).astype(bf16)
    ytmp[...] = jnp.zeros_like(ytmp)
    for k in range(4):
        tile = (k // 2) * (NZ + 1) * TY + (k % 2) * (NY + 1)
        ytmp[0:24, :] = acc[tile * 24 : tile * 24 + 24, :]
        sc[k] = join([ytmp[pl.ds(dx, 8, stride=4), :] for dx in range(4)])

    total = None
    for par in range(8):
        shift = (par // 4) * 128 + (par // 2 % 2) * 32 + par % 2
        part = jnp.concatenate(
            [gc[pl.ds(q * 512 + par, HID, stride=8), :] for q in range(4)], axis=1
        )
        part = pltpu.roll(part, 512 - shift, 1) if shift else part
        total = part if total is None else total + part
    total = total[:, :384]
    lane = iota((HID, 384), 1)
    dcol = jnp.sum(dsum[...], axis=1, keepdims=True)
    scol = jnp.sum(sqsum[...], axis=1, keepdims=True)
    total = jnp.where(lane == 28, dcol[:HID], total)
    total = jnp.where(lane == 29, dcol[HID:], total)
    total = jnp.where(lane == 30, scol[:HID] + scol[HID:], total)
    gc_out[...] = total


def compute(fields, halo, target, conv_w, conv_b, down_w, down_b):
    shapes = [
        ((OUT * 64, HX), bf16),
        ((C * NZ * NY, NX), f32),
        ((2, C * NY, NX), bf16),
        ((2, C * NZ, NX), bf16),
        ((4, 8, NX), f32),
        ((OUT, 512), f32),
        ((HID, 384), f32),
    ]
    scratch = [
        ((NX, 4 * HX), bf16),
        ((TZ * TY * 32, HX), f32),
        ((TZ * TY * 32, HX), bf16),
        ((OUT * 64, HX), f32),
        ((OUT * 64, HX), f32),
        ((512, 512), bf16),
        ((384, 512), bf16),
        ((512, OUT), bf16),
        ((4, 512, HX), f32),
        ((OUT, HX), f32),
        ((512, CELLS), f32),
        ((512, CELLS), bf16),
        ((512, CELLS), bf16),
        ((4 * 512, HX), f32),
        ((TZ * TY * 24, HX), f32),
        ((OUT, HX), f32),
        ((OUT, HX), f32),
        ((32, HX), f32),
    ]
    return pl.pallas_call(
        compute_kernel,
        out_shape=[jax.ShapeDtypeStruct(s, d) for s, d in shapes],
        in_specs=[VMEM] * 11,
        out_specs=[VMEM] * 7,
        scratch_shapes=[pltpu.VMEM(s, d) for s, d in scratch],
        compiler_params=pltpu.CompilerParams(vmem_limit_bytes=60 * 2**20),
        name="compute",
    )(
        fields, *halo, target.reshape(OUT * 64, HX), conv_w, conv_b.reshape(1, HID),
        down_w, down_b.reshape(1, OUT),
    )


def neighbour(dz, dy):
    nz, ny = lax.axis_size("gz"), lax.axis_size("gy")
    gz, gy = lax.axis_index("gz"), lax.axis_index("gy")
    return (lax.rem(gz + dz + nz, nz), lax.rem(gy + dy + ny, ny))


RIM = [(-1, 0), (1, 0), (0, -1), (0, 1), (-1, -1), (-1, 1), (1, -1), (1, 1)]


def greet(offsets):
    barrier = pltpu.get_barrier_semaphore()
    for dz, dy in offsets:
        pl.semaphore_signal(barrier, inc=1, device_id=neighbour(dz, dy), device_id_type=MESH)
    return lambda: pl.semaphore_wait(barrier, len(offsets))


def send(src, dst, sems, k, dz, dy):
    copy = pltpu.make_async_remote_copy(
        src_ref=src, dst_ref=dst, send_sem=sems.at[0, k], recv_sem=sems.at[1, k],
        device_id=neighbour(dz, dy), device_id_type=MESH,
    )
    copy.start()
    return copy


def halo_kernel(fields, zlo, zhi, ylo, yhi, corners, raw, ysend, csend, sems):
    wait = greet(RIM)
    for h in range(2):
        raw[h, 1536:2048, :] = jnp.zeros((512, HX), f32)
        for ch in range(C):
            for z in range(NZ):
                at = ch * 256 + z * NY
                raw[h, at : at + NY, :] = fields[ch, z, :, h * HX : (h + 1) * HX].astype(f32)
    for k, y in enumerate((0, NY - 1)):
        for h in range(2):
            ysend[k, :, h * HX : (h + 1) * HX] = raw[h, pl.ds(y, 48, stride=NY), :].astype(bf16)
    for k in range(4):
        at = (k // 2) * (NZ - 1) * NY + (k % 2) * (NY - 1)
        for h in range(2):
            csend[k, :, h * HX : (h + 1) * HX] = raw[h, pl.ds(at, 8, stride=256), :]
    wait()
    copies = [
        send(fields.at[:, NZ - 1], zlo, sems, 0, 1, 0),
        send(fields.at[:, 0], zhi, sems, 1, -1, 0),
        send(ysend.at[1], ylo, sems, 2, 0, 1),
        send(ysend.at[0], yhi, sems, 3, 0, -1),
    ]
    for k in range(4):
        dz, dy = 2 * (k // 2) - 1, 2 * (k % 2) - 1
        copies.append(send(csend.at[k], corners.at[3 - k], sems, 4 + k, dz, dy))
    for copy in copies:
        copy.wait()


def exchange_halo(fields):
    shapes = [
        ((C, NY, NX), bf16), ((C, NY, NX), bf16), ((C * NZ, NX), bf16), ((C * NZ, NX), bf16),
        ((4, 8, NX), f32),
    ]
    return pl.pallas_call(
        halo_kernel,
        out_shape=[jax.ShapeDtypeStruct(s, d) for s, d in shapes],
        in_specs=[VMEM],
        out_specs=[VMEM] * 5,
        scratch_shapes=[
            pltpu.VMEM((2, 2048, HX), f32),
            pltpu.VMEM((2, C * NZ, NX), bf16),
            pltpu.VMEM((4, 8, NX), f32),
            pltpu.SemaphoreType.DMA((2, 8)),
        ],
        compiler_params=pltpu.CompilerParams(collective_id=0, has_side_effects=True),
        name="halo",
    )(fields)


def reduce_kernel(
    nz, ny, sz, sy, sc, gd, gc, rz, ry, rc, gd_out, gc_out,
    gd_in, gc_in, gd_part, gc_part, gd_all, gc_all, gc_mine, sems,
):
    me_z, me_y = lax.axis_index("gz"), lax.axis_index("gy")
    peers = [(d, 0) for d in range(1, nz)] + [(0, d) for d in range(1, ny)]
    peers += [(dz, dy) for dz in (-1, 1) for dy in (-1, 1)]
    greet(peers)()
    first = []
    for d in range(1, nz):
        to = lax.rem(me_z + d, nz)
        rows = gd.at[pl.ds(pl.multiple_of(to * 8, 8), 8)]
        first.append(send(rows, gd_in.at[me_z], sems, d, d, 0))
    for d in range(1, ny):
        to = lax.rem(me_y + d, ny)
        rows = gc.at[pl.ds(pl.multiple_of(to * 8, 8), 8)]
        first.append(send(rows, gc_in.at[me_y], sems, nz + d, 0, d))
    k = nz + ny
    rims = [
        send(sz.at[0], rz.at[1], sems, k, -1, 0),
        send(sz.at[1], rz.at[0], sems, k + 1, 1, 0),
        send(sy.at[0], ry.at[1], sems, k + 2, 0, -1),
        send(sy.at[1], ry.at[0], sems, k + 3, 0, 1),
    ]
    for j in range(4):
        dz, dy = 2 * (j // 2) - 1, 2 * (j % 2) - 1
        rims.append(send(sc.at[j], rc.at[3 - j], sems, k + 4 + j, dz, dy))
    k += 8
    gd_in[me_z] = gd[pl.ds(pl.multiple_of(me_z * 8, 8), 8), :]
    gc_in[me_y] = gc[pl.ds(pl.multiple_of(me_y * 8, 8), 8), :]
    for copy in first:
        copy.wait()

    def added(ref, n):
        total = ref[0]
        for j in range(1, n):
            total = total + ref[j]
        return total

    gd_part[...] = added(gd_in, nz)
    gc_part[...] = added(gc_in, ny)
    second = [send(gd_part, gd_all.at[me_y], sems, k + d, 0, d) for d in range(1, ny)]
    k += ny
    second += [send(gc_part, gc_all.at[me_z], sems, k + d, d, 0) for d in range(1, nz)]
    k += nz
    gd_all[me_y] = gd_part[...]
    gc_all[me_z] = gc_part[...]
    for copy in second:
        copy.wait()
    gd_out[...] = added(gd_all, ny)
    gc_mine[...] = added(gc_all, nz)
    third = [send(gc_mine, gc_out.at[me_y], sems, k + d, 0, d) for d in range(1, ny)]
    gc_out[me_y] = gc_mine[...]
    for copy in third + rims:
        copy.wait()


def reduce_all(sz, sy, sc, gd, gc):
    nz, ny = lax.axis_size("gz"), lax.axis_size("gy")
    shapes = [
        (sz.shape, bf16), (sy.shape, bf16), (sc.shape, f32), ((8, 512), f32), ((8, 8, 384), f32),
    ]
    scratch = [
        (nz, 8, 512), (ny, 8, 384), (8, 512), (8, 384), (ny, 8, 512), (nz, 8, 384), (8, 384),
    ]
    return pl.pallas_call(
        functools.partial(reduce_kernel, nz, ny),
        out_shape=[jax.ShapeDtypeStruct(s, d) for s, d in shapes],
        in_specs=[VMEM] * 5,
        out_specs=[VMEM] * 5,
        scratch_shapes=[pltpu.VMEM(s, f32) for s in scratch]
        + [pltpu.SemaphoreType.DMA((2, 2 * nz + 3 * ny + 8))],
        compiler_params=pltpu.CompilerParams(collective_id=1, has_side_effects=True),
        name="reduce",
    )(sz, sy, sc, gd, gc)


def finish_kernel(cells, sens, rz, ry, rc, gd, gc, sens_out, conv, cbias, down, dbias, loss):
    row = iota((NY, NX), 0)
    sides = [ry[0].astype(f32), ry[1].astype(f32)]
    for ch in range(C):
        for z in range(NZ):
            i = ch * NZ + z
            value = sens[i * NY : (i + 1) * NY, :]
            low, high = sides[0][i : i + 1], sides[1][i : i + 1]
            if z in (0, NZ - 1):
                side = 0 if z == 0 else 1
                value = value + rz[side, ch * NY : (ch + 1) * NY, :].astype(f32)
                low = low + rc[2 * side, ch : ch + 1, :]
                high = high + rc[2 * side + 1, ch : ch + 1, :]
            value = value + jnp.where(row == 0, low, 0.0)
            value = value + jnp.where(row == NY - 1, high, 0.0)
            sens_out[i * NY : (i + 1) * NY, :] = value
    total = gc[...].reshape(HID, 384)
    exact = functools.partial(
        lax.dot_general, dimension_numbers=NT, preferred_element_type=f32,
        precision=lax.Precision.HIGHEST,
    )
    scale = 1.0 / cells
    conv[...] = exact(total, tap_matrix(384)) * scale
    lane, r = iota((8, 384), 1), iota((8, 384), 0)
    pick = one_hot(lane == jnp.where(r == 0, 24, r + 27))
    rows = exact(pick, total) * scale
    cbias[...] = rows[0:1]
    dbias[...] = rows[1:3]
    down[...] = gd[...] * scale
    square = jnp.where(iota((HID, 384), 1) == 30, total, 0.0)
    loss[...] = jnp.sum(square, keepdims=True) * (scale / OUT)


def finish(sens, rz, ry, rc, gd, gc):
    cells = 64 * HX * lax.axis_size("gz") * lax.axis_size("gy")
    shapes = [sens.shape, (HID, C * 27), (1, HID), (8, 512), (2, HID), (1, 1)]
    return pl.pallas_call(
        functools.partial(finish_kernel, cells),
        out_shape=[jax.ShapeDtypeStruct(s, f32) for s in shapes],
        in_specs=[VMEM] * 6,
        out_specs=[VMEM] * 6,
        name="finish",
    )(sens, rz, ry, rc, gd, gc)


def on_device(fields, target, conv_w, conv_b, down_w, down_b):
    halo = exchange_halo(fields)
    out, sens, sz, sy, sc, gd, gc = compute(fields, halo, target, conv_w, conv_b, down_w, down_b)
    rz, ry, rc, gd, gc = reduce_all(sz, sy, sc, gd, gc)
    sens, conv, cbias, down, dbias, loss = finish(sens, rz, ry, rc, gd, gc)
    return (
        out.reshape(target.shape),
        sens.reshape(fields.shape),
        conv,
        cbias.reshape(HID),
        down,
        dbias.reshape(OUT),
        loss.reshape(()),
    )


def solution(mesh):
    block = P(None, "gz", "gy", None)
    return jax.shard_map(
        on_device,
        mesh=mesh,
        in_specs=(block, block, P(), P(), P(), P()),
        out_specs=(block, block, P(), P(), P("gz", None), P(), P()),
        check_vma=False,
    )
```

time: 924 us -> 91.2 us (0.10); the launches traced: 907 us -> 91 us
  local copies, waits for them, and re-layouts: 477 us -> 1.26 us
  waiting for transfers between devices: 139 us -> 0 us
  Pallas kernels: 0 us -> 89.1 us
  matrix products: 86.2 us -> 0 us
  other arithmetic: 71.7 us -> 0 us
  blocking collectives: 69.3 us -> 0 us
  loops' own time: 31 us -> 0 us
  starting transfers between devices: 15.9 us -> 0 us
  between operations: 16.2 us -> 0.65 us
    while x288 -> x0, local copies, waits for them, and re-layouts: 133 us -> none
    psum x1 -> x0, waiting for transfers between devices: 130 us -> none  [on_device(): lax.psum((grad_down, grad_conv, grad_cbias, grad_dbias, square_sum), ('gz...]
    pallas_call x0 -> x4, Pallas kernels: none -> 89.1 us  [the longest x1 44.8 us: compute(): pl.pallas_call(compute_kernel, out_shape=[jax.ShapeDtypeStruct(s, d) for...]
    dot_general x24 -> x0, matrix products: 86.2 us -> none  [the longest x4 29.3 us: pair_step(): jnp.dot(conv_weight, columns, preferred_element_type=jnp.float32)]
    psum x1 -> x0, blocking collectives: 69.3 us -> none  [on_device(): lax.psum((grad_down, grad_conv, grad_cbias, grad_dbias, square_sum), ('gz...]
    reshape x12 -> x1, local copies, waits for them, and re-layouts: 68.2 us -> 1.26 us  [on_device(): dbias.reshape(OUT)]
    slice x421 -> x0, local copies, waits for them, and re-layouts: 66.2 us -> none  [the longest x288 22.9 us: parity_window(): piece = jnp.roll(piece, col_step, axis=2)]
    unnamed x13 -> x0, local copies, waits for them, and re-layouts: 59.6 us -> none
  transfers between devices with their start and end apart: 9 -> 0, of which waited for: 6 -> 0; matrix products, arithmetic and copies ran while one was open for 9% -> 0% of each run, Pallas kernels for 0% -> 0%
where the time goes in v1:
time: 91.2 us; the launch traced here: 91 us
  Pallas kernels  89.1 us (98%)
  local copies, waits for them, and re-layouts  1.26 us (1%)
    pallas_call x1, Pallas kernels, compute(): pl.pallas_call(compute_kernel, out_shape=[jax.ShapeDtypeStruct(s, d) for...  44.8 us
    pallas_call x1, Pallas kernels, reduce_all(): pl.pallas_call(functools.partial(reduce_kernel, nz, ny), out_shape=[jax.S...  26.4 us
    pallas_call x1, Pallas kernels, exchange_halo(): pl.pallas_call(halo_kernel, out_shape=[jax.ShapeDtypeStruct(s, d) for s,...  14.5 us
    pallas_call x1, Pallas kernels, finish(): pl.pallas_call(functools.partial(finish_kernel, cells), out_shape=[jax.Sh...  3.34 us

profile of v1, /device:TPU:0, one launch (start us, length us, event | category | flops | bytes accessed | tf_op | source)
XLA Modules:
  0.0 91.0 jit_solution(3617320456528848722)
XLA Ops:
  0.6 14.5 %halo.1 = (bf16[6,32,256]{2,1,0:T(8,128)(2,1)}, bf16[6,32,256]{2,1,0:T(8,128)(2,1)}, bf16[48,256]{1,0:T(8,128)(2,1)}, bf16[48,256]{1,0:T(8,128)(2,1)}, f32[4,8,256]{2,1,0:T(8,128)}) custom-call(bf16[6,8,32,256]{3,2,1,0:T(8,128)(2,1)} %fields.3), custom_call_target="tpu_custom_call" | custom-call | tf_op jit(solution)/shard_map/halo/pallas_call | solution.py:361
  15.1 44.8 %compute.1 = (bf16[8192,128]{1,0:T(8,128)(2,1)}, f32[1536,256]{1,0:T(8,128)}, bf16[2,192,256]{2,1,0:T(8,128)(2,1)}, bf16[2,48,256]{2,1,0:T(8,128)(2,1)}, f32[4,8...) custom-call(bf16[6,8,32,256]{3,2,1,0:T(8,128)(2,1)} %fields.3, bf16[6,32,256]{2,1,0:T(8,128)(2,1)} %get-tuple-element.30.zlo, ...), custom_call_target="tpu_custom_call" | custom-call | tf_op jit(solution)/shard_map/compute/pallas_call | solution.py:288
  60.0 26.4 %reduce.1 = (bf16[2,192,256]{2,1,0:T(8,128)(2,1)}, bf16[2,48,256]{2,1,0:T(8,128)(2,1)}, f32[4,8,256]{2,1,0:T(8,128)}, f32[8,512]{1,0:T(8,128)}, f32[8,8,384]{2,1,0:T(8,128)}) custom-call(bf16[2,192,256]{2,1,0:T(8,128)(2,1)} %get-tuple-element.37.sz, bf16[2,48,256]{2,1,0:T(8,128)(2,1)} %get-tuple-element.38.sy, f32[4,8,256]{2,1,0:T(8,128)} %get-tuple-element.39.sc, ...), custom_call_target="tpu_custom_call" | custom-call | tf_op jit(solution)/shard_map/reduce/pallas_call | solution.py:442
  86.4 3.3 %finish.1 = (f32[1536,256]{1,0:T(8,128)}, f32[64,162]{1,0:T(8,128)}, f32[1,64]{1,0:T(1,128)}, f32[8,512]{1,0:T(8,128)}, f32[2,64]{1,0:T(2,128)}, /*index=5*/f32[1,1]{1,0:T(1,128)}) custom-call(f32[1536,256]{1,0:T(8,128)} %get-tuple-element.36.sens, bf16[2,192,256]{2,1,0:T(8,128)(2,1)} %get-tuple-element.42.rz, bf16[2,48,256]{2,1,0:T(8,128)(2,1)} %get-tuple-element.43.ry, ...), custom_call_target="tpu_custom_call" | custom-call | tf_op jit(solution)/shard_map/finish/pallas_call | solution.py:490
  89.7 1.3 %reshape.44 = f32[128]{0:T(128)} reshape(f32[2,64]{1,0:T(2,128)} %get-tuple-element.51) | data formatting | bytes 1024 | tf_op jit(solution)/shard_map/reshape | solution.py:510
